TPU v7x, 512 devices: a whole 4x4x16 slice. The times are simulated.
512 devices in a mesh: dp: 32 (over x, y, core), expert: 16 (over z).
Axes of the slice: x: 4, y: 4, z: 16, core: 2. Of those that a mesh axis runs over, the one named last changes fastest.
Arguments:
- tokens: bfloat16 [65536, 7168], P(('dp', 'expert')), may hold values from -6 to 6
- route_ids: int32 [65536, 8], P(('dp', 'expert')), may hold values from 0 to 255, as said below
- route_gates: float32 [65536, 8], P(('dp', 'expert')), may hold values from 0.1 to 1
- gate_up: bfloat16 [2, 7168, 2048], P(None, 'dp', 'expert'), may hold values from -0.0625 to 0.0625
- down_weight: bfloat16 [2048, 7168], P('expert', 'dp'), may hold values from -0.125 to 0.125
Outputs:
- mixed: bfloat16 [65536, 7168], P(('dp', 'expert'))
Inputs may be any that keep to these rules, and one draw needn't show every extreme that they name: `route_ids`: each token names 8 different experts. Among the 128 rows of one device, each expert below 1 is named by 1 to 12 rows; for each such expert, in every draw some run of 16 consecutive devices' blocks (aligned at multiples of 16) has exactly 12 rows naming it in every block.
All inputs are finite; a program needn't handle non-finite values.
Results may differ from a plain program's by a relative error of at most 0.0057.
Values may be sent and summed in bfloat16 or wider, within the bound.
No kernel may reach another device: no remote copies, remote signals or barrier semaphores. Data moves between devices by JAX's collectives and lax.ppermute only.
A program may use at most 64 MiB of HBM per device.

v0:
```python
import jax
import jax.numpy as jnp
from jax import lax
from jax.sharding import PartitionSpec as P

EXPERTS = 1
CAP = 12


def partner_2(block, axis, bit):
    count = lax.axis_size(axis)
    route = []
    for low in range(count):
        high = low | 1 << bit
        if high != low and high < count:
            route += [(low, high), (high, low)]
    return lax.ppermute(block, axis, route)


def spread_rounds(buffer, members):
    depth = buffer.shape[1]
    model_width = buffer.shape[2]
    for level in range(members.bit_length() - 1):
        shaped = buffer.reshape(members >> level + 1, 2, 1 << level, depth, model_width)
        partner = partner_2(shaped[:, 1], "expert", level)
        shaped = jnp.stack((shaped[:, 0], partner), axis=1)
        buffer = shaped.reshape(members, depth, model_width)
    return buffer


def collect_rounds(buffer, members):
    depth = buffer.shape[1]
    model_width = buffer.shape[2]
    for level in reversed(range(members.bit_length() - 1)):
        shaped = buffer.reshape(members >> level + 1, 2, 1 << level, depth, model_width)
        partner = partner_2(shaped[:, 1], "expert", level)
        shaped = jnp.stack((shaped[:, 0], partner), axis=1)
        buffer = shaped.reshape(members, depth, model_width)
    return buffer


def body(tokens, route_ids, route_gates, gate_up, down_weight):
    members = lax.axis_size("expert")
    slices = members // EXPERTS
    model_width = tokens.shape[1]
    window_ids = jnp.arange(EXPERTS, dtype=jnp.int32)
    matches = route_ids[:, :, None] == window_ids[None, None, :]
    routed = jnp.any(matches, axis=1)
    weight = jnp.sum(jnp.where(matches, route_gates[:, :, None], 0.0), axis=1)
    places = jnp.cumsum(routed.astype(jnp.int32), axis=0) - 1
    capacity_ids = jnp.arange(CAP, dtype=jnp.int32)
    packing = (routed[None, :, :] & (places[None, :, :] == capacity_ids[:, None, None])).astype(
        jnp.bfloat16
    )
    packed = jnp.einsum("cte,td->ecd", packing, tokens, preferred_element_type=jnp.float32).astype(
        jnp.bfloat16
    )
    outgoing = jnp.broadcast_to(packed[:, None], (EXPERTS, slices, CAP, model_width)).reshape(
        members, CAP, model_width
    )
    relative = jnp.bitwise_xor(jnp.arange(members, dtype=jnp.int32), lax.axis_index("expert"))
    incoming = spread_rounds(jnp.take(outgoing, relative, axis=0), members)
    dispatched = incoming.reshape(members * CAP, model_width)
    projected = jnp.einsum(
        "rd,gdf->grf",
        dispatched,
        lax.all_gather(gate_up, "dp", axis=1, tiled=True),
        preferred_element_type=jnp.float32,
    )
    hidden = (jax.nn.silu(projected[0]) * projected[1]).astype(jnp.bfloat16)
    partial_value = jnp.dot(
        hidden,
        lax.all_gather(down_weight, "dp", axis=1, tiled=True),
        preferred_element_type=jnp.float32,
    ).astype(jnp.bfloat16)
    returning = partial_value.reshape(members, CAP, model_width)
    returned = jnp.take(collect_rounds(returning, members), relative, axis=0)
    summed = jnp.sum(
        returned.reshape(EXPERTS, slices, CAP, model_width).astype(jnp.float32), axis=1
    )
    selector = routed & (places == capacity_ids[None, :])
    scaled = jnp.where(selector, weight, 0.0)
    mixed = jnp.dot(
        scaled, summed[0], precision=lax.Precision.HIGHEST, preferred_element_type=jnp.float32
    )
    return mixed.astype(jnp.bfloat16)


def solution(mesh):
    return jax.shard_map(
        body,
        mesh=mesh,
        in_specs=(
            P(("dp", "expert"), None),
            P(("dp", "expert"), None),
            P(("dp", "expert"), None),
            P(None, "dp", "expert"),
            P("expert", "dp"),
        ),
        out_specs=P(("dp", "expert"), None),
        check_vma=False,
    )
```

profile of v0, /device:TPU:1, one launch (start us, length us, event | category | flops | bytes accessed | tf_op | source)
XLA Modules:
  0.0 816.3 jit_solution(7041955684502544841)
XLA Ops:
  10.6 4.6 gather_fusion
  21.1 4.4 collective-permute-start
  29.0 22.3 %collective-permute-done = bf16[8,1,12,7168]{3,0,2,1:T(8,128)(2,1)} collective-permute-done((bf16[8,1,12,7168]{3,0,2,1:T(8,128)(2,1)}, bf16[8,1,12,7168]{3,0,2,1:T(8,128)(2,1)}, u32[]{:S(2)}, u32[]{:S(2)}) %collective-permute-start) | collective-permute-done | bytes 1376288 | tf_op jit(solution)/shard_map/ppermute | solution.py:17
  51.2 4.0 stack.53
  57.8 6.1 fusion.20
  66.1 9.4 %collective-permute-start.1 = (bf16[4,2,12,7168]{3,1,2,0:T(2,128)(2,1)S(1)}, bf16[4,2,12,7168]{3,1,2,0:T(2,128)(2,1)S(1)}, u32[]{:S(2)}, u32[]{:S(2)}) collective-permute-start(bf16[4,2,12,7168]{3,1,2,0:T(2,128)(2,1)S(1)} %bitcast.83), channel_id=1, source_target_pairs={{0,2},{2,0},{1,3},{3,1},{4,6},{6,4},{5,7},{7,5},{8,10},{10,8},{9,1... | collective-permute-start | bytes 4128776 | tf_op jit(solution)/shard_map/ppermute | solution.py:17
  75.5 59.0 %collective-permute-done.1 = bf16[4,2,12,7168]{3,1,2,0:T(2,128)(2,1)S(1)} collective-permute-done((bf16[4,2,12,7168]{3,1,2,0:T(2,128)(2,1)S(1)}, bf16[4,2,12,7168]{3,1,2,0:T(2,128)(2,1)S(1)}, u32[]{:S(2)}, u32[]{:S(2)}) %collective-permute-start.1) | collective-permute-done | bytes 1376288 | tf_op jit(solution)/shard_map/ppermute | solution.py:17
  137.3 6.2 pad_maximum_fusion
  143.5 4.4 copy.78
  147.9 6.4 reshape_reshape.20
  157.0 8.8 %collective-permute-start.2 = (bf16[2,4,12,7168]{3,1,2,0:T(4,128)(2,1)}, bf16[2,4,12,7168]{3,1,2,0:T(4,128)(2,1)S(1)}, u32[]{:S(2)}, u32[]{:S(2)}) collective-permute-start(bf16[2,4,12,7168]{3,1,2,0:T(4,128)(2,1)} %get-tuple-element.21), channel_id=1, source_target_pairs={{0,4},{4,0},{1,5},{5,1},{2,6},{6,2},{3,7},{7,3},{8,12},{12,8},{9,1... | collective-permute-start | bytes 4128776 | tf_op jit(solution)/shard_map/ppermute | solution.py:17
  165.9 148.0 %collective-permute-done.2 = bf16[2,4,12,7168]{3,1,2,0:T(4,128)(2,1)S(1)} collective-permute-done((bf16[2,4,12,7168]{3,1,2,0:T(4,128)(2,1)}, bf16[2,4,12,7168]{3,1,2,0:T(4,128)(2,1)S(1)}, u32[]{:S(2)}, u32[]{:S(2)}) %collective-permute-start.2) | collective-permute-done | bytes 1376288 | tf_op jit(solution)/shard_map/ppermute | solution.py:17
  313.9 3.4 pad_maximum_fusion.1
  320.1 4.9 fusion.19
  326.5 102.3 %collective-permute-start.3 = (bf16[1,8,12,7168]{3,1,2,0:T(8,128)(2,1)S(1)}, bf16[1,8,12,7168]{3,1,2,0:T(8,128)(2,1)S(1)}, u32[]{:S(2)}, u32[]{:S(2)}) collective-permute-start(bf16[1,8,12,7168]{3,1,2,0:T(8,128)(2,1)S(1)} %bitcast.85), channel_id=1, source_target_pairs={{0,8},{8,0},{1,9},{9,1},{2,10},{10,2},{3,11},{11,3},{4,12},{12,4},... | collective-permute-start | bytes 4128776 | tf_op jit(solution)/shard_map/ppermute | solution.py:17
  428.8 59.2 %collective-permute-done.3 = bf16[1,8,12,7168]{3,1,2,0:T(8,128)(2,1)S(1)} collective-permute-done((bf16[1,8,12,7168]{3,1,2,0:T(8,128)(2,1)S(1)}, bf16[1,8,12,7168]{3,1,2,0:T(8,128)(2,1)S(1)}, u32[]{:S(2)}, u32[]{:S(2)}) %collective-permute-start.3) | collective-permute-done | bytes 1376288 | tf_op jit(solution)/shard_map/ppermute | solution.py:17
  490.1 6.2 pad_maximum_fusion.2
  498.9 3.2 reshape.119
  513.2 6.0 collective-permute-start.4
  520.2 34.1 %collective-permute-done.4 = bf16[1,8,12,7168]{3,1,2,0:T(8,128)(2,1)} collective-permute-done((bf16[1,8,12,7168]{3,1,2,0:T(8,128)(2,1)S(1)}, bf16[1,8,12,7168]{3,1,2,0:T(8,128)(2,1)}, u32[]{:S(2)}, u32[]{:S(2)}) %collective-permute-start.4) | collective-permute-done | bytes 1376288 | tf_op jit(solution)/shard_map/ppermute | solution.py:17
  554.3 3.5 stack.62
  560.7 59.4 %collective-permute-start.5 = (bf16[2,4,12,7168]{3,1,2,0:T(4,128)(2,1)S(1)}, bf16[2,4,12,7168]{3,1,2,0:T(4,128)(2,1)S(1)}, u32[]{:S(2)}, u32[]{:S(2)}) collective-permute-start(bf16[2,4,12,7168]{3,1,2,0:T(4,128)(2,1)S(1)} %get-tuple-element.17), channel_id=1, source_target_pairs={{0,4},{4,0},{1,5},{5,1},{2,6},{6,2},{3,7},{7,3},{8,12},{12,8},{9,1... | collective-permute-start | bytes 4128776 | tf_op jit(solution)/shard_map/ppermute | solution.py:17
  620.1 52.2 %collective-permute-done.5 = bf16[2,4,12,7168]{3,1,2,0:T(4,128)(2,1)S(1)} collective-permute-done((bf16[2,4,12,7168]{3,1,2,0:T(4,128)(2,1)S(1)}, bf16[2,4,12,7168]{3,1,2,0:T(4,128)(2,1)S(1)}, u32[]{:S(2)}, u32[]{:S(2)}) %collective-permute-start.5) | collective-permute-done | bytes 1376288 | tf_op jit(solution)/shard_map/ppermute | solution.py:17
  672.3 3.5 pad_maximum_fusion.3
  675.8 5.5 reshape_reshape.24
  685.5 55.2 %collective-permute-done.6 = bf16[4,2,12,7168]{3,1,2,0:T(2,128)(2,1)S(1)} collective-permute-done((bf16[4,2,12,7168]{3,1,2,0:T(2,128)(2,1)S(1)}, bf16[4,2,12,7168]{3,1,2,0:T(2,128)(2,1)S(1)}, u32[]{:S(2)}, u32[]{:S(2)}) %collective-permute-start.6) | collective-permute-done | bytes 1376288 | tf_op jit(solution)/shard_map/ppermute | solution.py:17
  740.7 3.9 pad_maximum_fusion.4
  746.5 4.9 fusion.18
  755.1 31.0 %collective-permute-done.7 = bf16[8,1,12,7168]{3,0,2,1:T(8,128)(2,1)S(1)} collective-permute-done((bf16[8,1,12,7168]{3,0,2,1:T(8,128)(2,1)S(1)}, bf16[8,1,12,7168]{3,0,2,1:T(8,128)(2,1)S(1)}, u32[]{:S(2)}, u32[]{:S(2)}) %collective-permute-start.7) | collective-permute-done | bytes 1376288 | tf_op jit(solution)/shard_map/ppermute | solution.py:17
  788.2 6.2 pad_maximum_fusion.5
  797.0 4.8 gather_fusion.1
  804.8 4.2 convolution_convert_fusion.1
  (49 shorter events, 64.8 us)
Async XLA Ops:
  6.5 1.5 copy-start
  6.5 495.6 %all-gather.3.cloned.1.call-start = ((), (), s32[]{:S(2)}) async-start(), calls=%async_computation | async-start | bytes 3784704 | tf_op jit(solution)/shard_map/all_gather | solution.py:67
  21.1 30.1 %collective-permute-start = (bf16[8,1,12,7168]{3,0,2,1:T(8,128)(2,1)}, bf16[8,1,12,7168]{3,0,2,1:T(8,128)(2,1)}, u32[]{:S(2)}, u32[]{:S(2)}) collective-permute-start(bf16[8,1,12,7168]{3,0,2,1:T(8,128)(2,1)} %bitcast.70), channel_id=1, source_target_pairs={{0,1},{1,0},{2,3},{3,2},{4,5},{5,4},{6,7},{7,6},{8,9},{9,8},{10,11... | collective-permute-start | bytes 4128776 | tf_op jit(solution)/shard_map/ppermute | solution.py:17
  25.5 479.6 %all-gather.5.cloned.1.call-start = ((), (), s32[]{:S(2)}) async-start(), calls=%async_computation.1 | async-start | bytes 1892352 | tf_op jit(solution)/shard_map/all_gather | solution.py:73
  66.1 68.4 %collective-permute-start.1 = (bf16[4,2,12,7168]{3,1,2,0:T(2,128)(2,1)S(1)}, bf16[4,2,12,7168]{3,1,2,0:T(2,128)(2,1)S(1)}, u32[]{:S(2)}, u32[]{:S(2)}) collective-permute-start(bf16[4,2,12,7168]{3,1,2,0:T(2,128)(2,1)S(1)} %bitcast.83), channel_id=1, source_target_pairs={{0,2},{2,0},{1,3},{3,1},{4,6},{6,4},{5,7},{7,5},{8,10},{10,8},{9,1... | collective-permute-start | bytes 4128776 | tf_op jit(solution)/shard_map/ppermute | solution.py:17
  157.0 156.8 %collective-permute-start.2 = (bf16[2,4,12,7168]{3,1,2,0:T(4,128)(2,1)}, bf16[2,4,12,7168]{3,1,2,0:T(4,128)(2,1)S(1)}, u32[]{:S(2)}, u32[]{:S(2)}) collective-permute-start(bf16[2,4,12,7168]{3,1,2,0:T(4,128)(2,1)} %get-tuple-element.21), channel_id=1, source_target_pairs={{0,4},{4,0},{1,5},{5,1},{2,6},{6,2},{3,7},{7,3},{8,12},{12,8},{9,1... | collective-permute-start | bytes 4128776 | tf_op jit(solution)/shard_map/ppermute | solution.py:17
  326.5 161.5 %collective-permute-start.3 = (bf16[1,8,12,7168]{3,1,2,0:T(8,128)(2,1)S(1)}, bf16[1,8,12,7168]{3,1,2,0:T(8,128)(2,1)S(1)}, u32[]{:S(2)}, u32[]{:S(2)}) collective-permute-start(bf16[1,8,12,7168]{3,1,2,0:T(8,128)(2,1)S(1)} %bitcast.85), channel_id=1, source_target_pairs={{0,8},{8,0},{1,9},{9,1},{2,10},{10,2},{3,11},{11,3},{4,12},{12,4},... | collective-permute-start | bytes 4128776 | tf_op jit(solution)/shard_map/ppermute | solution.py:17
  513.2 41.2 %collective-permute-start.4 = (bf16[1,8,12,7168]{3,1,2,0:T(8,128)(2,1)S(1)}, bf16[1,8,12,7168]{3,1,2,0:T(8,128)(2,1)}, u32[]{:S(2)}, u32[]{:S(2)}) collective-permute-start(bf16[1,8,12,7168]{3,1,2,0:T(8,128)(2,1)S(1)} %copy.84), channel_id=1, source_target_pairs={{0,8},{8,0},{1,9},{9,1},{2,10},{10,2},{3,11},{11,3},{4,12},{12,4},... | collective-permute-start | bytes 4128776 | tf_op jit(solution)/shard_map/ppermute | solution.py:17
  560.7 111.6 %collective-permute-start.5 = (bf16[2,4,12,7168]{3,1,2,0:T(4,128)(2,1)S(1)}, bf16[2,4,12,7168]{3,1,2,0:T(4,128)(2,1)S(1)}, u32[]{:S(2)}, u32[]{:S(2)}) collective-permute-start(bf16[2,4,12,7168]{3,1,2,0:T(4,128)(2,1)S(1)} %get-tuple-element.17), channel_id=1, source_target_pairs={{0,4},{4,0},{1,5},{5,1},{2,6},{6,2},{3,7},{7,3},{8,12},{12,8},{9,1... | collective-permute-start | bytes 4128776 | tf_op jit(solution)/shard_map/ppermute | solution.py:17
  683.3 57.4 %collective-permute-start.6 = (bf16[4,2,12,7168]{3,1,2,0:T(2,128)(2,1)S(1)}, bf16[4,2,12,7168]{3,1,2,0:T(2,128)(2,1)S(1)}, u32[]{:S(2)}, u32[]{:S(2)}) collective-permute-start(bf16[4,2,12,7168]{3,1,2,0:T(2,128)(2,1)S(1)} %get-tuple-element.15), channel_id=1, source_target_pairs={{0,2},{2,0},{1,3},{3,1},{4,6},{6,4},{5,7},{7,5},{8,10},{10,8},{9,1... | collective-permute-start | bytes 4128776 | tf_op jit(solution)/shard_map/ppermute | solution.py:17
  752.9 33.2 %collective-permute-start.7 = (bf16[8,1,12,7168]{3,0,2,1:T(8,128)(2,1)S(1)}, bf16[8,1,12,7168]{3,0,2,1:T(8,128)(2,1)S(1)}, u32[]{:S(2)}, u32[]{:S(2)}) collective-permute-start(bf16[8,1,12,7168]{3,0,2,1:T(8,128)(2,1)S(1)} %bitcast.87), channel_id=1, source_target_pairs={{0,1},{1,0},{2,3},{3,2},{4,5},{5,4},{6,7},{7,6},{8,9},{9,8},{10,11... | collective-permute-start | bytes 4128776 | tf_op jit(solution)/shard_map/ppermute | solution.py:17
  797.0 12.0 %copy-start.1 = (bf16[128,7168]{1,0:T(8,128)(2,1)S(1)}, bf16[128,7168]{1,0:T(8,128)(2,1)}, u32[]{:S(2)}) copy-start(bf16[128,7168]{1,0:T(8,128)(2,1)} %param.7) | copy-start | bytes 5505028
Sparse Core Ops, SparseCore 0:
  25.6 65.0 all-gather.2
  166.0 58.7 all-gather.4
where the time goes:
time: 820 us; the launch traced here: 816 us
  waiting for transfers between devices  461 us (56%)
  starting transfers between devices  195 us (24%)
  local copies, waits for them, and re-layouts  100 us (12%)
  other arithmetic  36.2 us (4%)
  between operations  14.2 us (2%)
  matrix products  9.86 us (1%)
    ppermute x8, waiting for transfers between devices, partner_2(): return lax.ppermute(block, axis, route)  461 us
    ppermute x8, starting transfers between devices, partner_2(): return lax.ppermute(block, axis, route)  195 us
    another operation x7, local copies, waits for them, and re-layouts, spread_rounds(): shaped = jnp.stack((shaped[:, 0], partner), axis=1)  21.3 us
  transfers between devices with their start and end apart: 10, of which 8 were waited for; matrix products, arithmetic and copies ran while one was open for 9% of the time, Pallas kernels for 0%

commit v1 on v0

v1 whole, which is shorter than its diff:
```python
import jax
import jax.numpy as jnp
from jax import lax
from jax.sharding import PartitionSpec as P

EXPERTS = 1
CAP = 12


def body(tokens, route_ids, route_gates, gate_up, down_weight):
    model_width = tokens.shape[1]
    matches = route_ids == 0
    routed = jnp.any(matches, axis=1)
    weight = jnp.sum(jnp.where(matches, route_gates, 0.0), axis=1)
    places = jnp.cumsum(routed.astype(jnp.int32)) - 1
    capacity_ids = jnp.arange(CAP, dtype=jnp.int32)
    packing = (routed[None, :] & (places[None, :] == capacity_ids[:, None])).astype(jnp.bfloat16)
    packed = jnp.dot(packing, tokens, preferred_element_type=jnp.float32).astype(jnp.bfloat16)
    dispatched = lax.all_gather(packed, "expert", axis=0, tiled=True)
    gu = lax.all_gather(gate_up, "dp", axis=1, tiled=True)
    dn = lax.all_gather(down_weight, "dp", axis=1, tiled=True)
    projected = jnp.einsum("rd,gdf->grf", dispatched, gu, preferred_element_type=jnp.float32)
    hidden = (jax.nn.silu(projected[0]) * projected[1]).astype(jnp.bfloat16)
    partial_value = jnp.dot(hidden, dn, preferred_element_type=jnp.float32).astype(jnp.bfloat16)
    summed = lax.psum_scatter(partial_value, "expert", scatter_dimension=0, tiled=True)
    selector = routed[:, None] & (places[:, None] == capacity_ids[None, :])
    scaled = jnp.where(selector, weight[:, None], 0.0)
    mixed = jnp.dot(
        scaled, summed.astype(jnp.float32), precision=lax.Precision.HIGHEST, preferred_element_type=jnp.float32
    )
    return mixed.astype(jnp.bfloat16)


def solution(mesh):
    return jax.shard_map(
        body,
        mesh=mesh,
        in_specs=(
            P(("dp", "expert"), None),
            P(("dp", "expert"), None),
            P(("dp", "expert"), None),
            P(None, "dp", "expert"),
            P("expert", "dp"),
        ),
        out_specs=P(("dp", "expert"), None),
        check_vma=False,
    )
```

time: 820 us -> 335 us (0.41)
  the two profiles are of different devices: /device:TPU:1 before, /device:TPU:96 now
where the time goes in v1:
time: 335 us
  waiting for transfers between devices  227 us (68%)
  blocking collectives  46.2 us (14%)
  starting transfers between devices  19.2 us (6%)
  local copies, waits for them, and re-layouts  15.3 us (5%)
  between operations  13.8 us (4%)
  matrix products  11.6 us (3%)
    all_gather x1, waiting for transfers between devices, body(): dispatched = lax.all_gather(packed, 'expert', axis=0, tiled=True)  78.2 us
    all_gather x1, waiting for transfers between devices, body(): dn = lax.all_gather(down_weight, 'dp', axis=1, tiled=True)  57.5 us
    all_gather x1, waiting for transfers between devices, body(): gu = lax.all_gather(gate_up, 'dp', axis=1, tiled=True)  57.5 us
    unnamed x1, blocking collectives  46.2 us
    unnamed x7, waiting for transfers between devices  34.1 us
    unnamed x4, starting transfers between devices  19.1 us
    unnamed x10, local copies, waits for them, and re-layouts  15.2 us
  transfers between devices with their start and end apart: 7, of which 4 were waited for; matrix products, arithmetic and copies ran while one was open for 3% of the time, Pallas kernels for 0%

profile of v1, /device:TPU:96, one launch (start us, length us, event | category | flops | bytes accessed | tf_op | source)
XLA Modules:
  0.0 334.5 jit_solution(3972932187216507593)
XLA Ops:
  6.5 0.9 select_reduce_fusion
  7.4 0.1 copy.8
  7.5 0.2 reduce-window.7
  7.7 0.1 add_reduce_fusion
  7.8 0.3 copy-done
  8.1 1.0 fusion.1
  9.1 0.0 all-gather.9.cloned.1.call-update
  9.1 0.0 all-gather.5.cloned.1.call-start
  9.2 0.7 all-gather.5.cloned.1.call-update
  9.9 0.0 all-gather.7.cloned.1.call-start
  9.9 0.7 all-gather.7.cloned.1.call-update
  10.6 78.2 %all-gather.9.cloned.1.call-done = bf16[16,12,7168]{2,1,0:T(8,128)(2,1)} async-done(((bf16[1,12,7168]{2,1,0:T(8,128)(2,1)}), bf16[16,12,7168]{2,1,0:T(8,128)(2,1)}) %all-gather.9.cloned.1.call-update) | async-done | bytes 2752528 | tf_op jit(solution)/shard_map/all_gather | solution.py:19
  88.8 4.5 %reshape.35 = bf16[192,7168,1]{1,0,2:T(8,128)(2,1)} reshape(bf16[16,12,7168]{2,1,0:T(8,128)(2,1)} %all-gather.9.cloned.1.call-done) | data formatting | bytes 5505024
  93.3 57.5 %all-gather.5.cloned.1.call-done = bf16[2,7168,128]{2,1,0:T(8,128)(2,1)} async-done(((bf16[2,224,128]{2,1,0:T(8,128)(2,1)}), bf16[2,7168,128]{2,1,0:T(8,128)(2,1)}) %all-gather.5.cloned.1.call-update) | async-done | bytes 3670032 | tf_op jit(solution)/shard_map/all_gather | solution.py:20
  150.7 3.8 %convolution_bitcast_fusion = f32[2,192,128]{2,1,0:T(8,128)S(1)} fusion(bf16[192,7168,1]{1,0,2:T(8,128)(2,1)} %reshape.35, bf16[2,7168,128]{2,1,0:T(8,128)(2,1)} %all-gather.5.cloned.1.call-done), kind=kOutput, calls=%fused_computation.4 | convolution fusion | flops 704643072 | bytes 6619136 | tf_op jit(solution)/shard_map/rd,gdf->grf/dot_general | solution.py:22
  154.5 57.5 %all-gather.7.cloned.1.call-done = bf16[128,7168]{0,1:T(8,128)(2,1)} async-done(((bf16[128,224]{0,1:T(8,128)(2,1)}), bf16[128,7168]{0,1:T(8,128)(2,1)}) %all-gather.7.cloned.1.call-update) | async-done | bytes 1835024 | tf_op jit(solution)/shard_map/all_gather | solution.py:21
  212.0 3.9 %convolution_convert_fusion = bf16[192,7168]{1,0:T(8,128)(2,1)} fusion(bf16[128,7168]{0,1:T(8,128)(2,1)} %all-gather.7.cloned.1.call-done, f32[2,192,128]{2,1,0:T(8,128)S(1)} %convolution_bitcast_fusion), kind=kOutput, calls=%fused_computation | convolution fusion | flops 353845248 | bytes 4784128 | tf_op jit(solution)/shard_map/dot_general | solution.py:24
  215.9 46.2 %fusion = bf16[16,7168]{1,0:T(8,128)(2,1)S(1)} fusion(bf16[192,7168]{1,0:T(8,128)(2,1)} %convolution_convert_fusion), kind=kCustom, calls=%all-reduce-scatter | all-reduce-scatter fusion | flops 1835009 | bytes 2983936
  262.1 5.4 %collective-permute-start = (bf16[16,7168]{1,0:T(8,128)(2,1)S(1)}, bf16[16,7168]{1,0:T(8,128)(2,1)S(1)}, u32[]{:S(2)}, u32[]{:S(2)}) collective-permute-start(bf16[16,7168]{1,0:T(8,128)(2,1)S(1)} %fusion), channel_id=1, source_target_pairs={{0,1},{1,2},{2,3},{3,4},{4,5},{5,6},{6,7},{7,8},{8,9},{9,10},{10,1... | collective-permute-start | bytes 688136
  267.6 2.4 collective-permute-start.1
  270.0 6.7 %collective-permute-start.2 = (bf16[16,7168]{1,0:T(8,128)(2,1)S(1)}, bf16[16,7168]{1,0:T(8,128)(2,1)}, u32[]{:S(2)}, u32[]{:S(2)}) collective-permute-start(bf16[16,7168]{1,0:T(8,128)(2,1)S(1)} %fusion), channel_id=1, source_target_pairs={{0,3},{1,4},{2,5},{3,6},{4,7},{5,8},{6,9},{7,10},{8,11},{9,12},{10... | collective-permute-start | bytes 688136
  276.7 0.1 slice.10
  276.7 4.6 %collective-permute-start.3 = (bf16[12,7168]{1,0:T(8,128)(2,1)S(1)}, bf16[12,7168]{1,0:T(8,128)(2,1)S(1)}, u32[]{:S(2)}, u32[]{:S(2)}) collective-permute-start(bf16[12,7168]{1,0:T(8,128)(2,1)S(1)} %slice.10), channel_id=1, source_target_pairs={{0,4},{1,5},{2,6},{3,7},{4,8},{5,9},{6,10},{7,11},{8,12},{9,13},{1... | collective-permute-start | bytes 516104
  281.3 1.3 dynamic-slice.4
  283.2 32.7 %collective-permute-done.3 = bf16[12,7168]{1,0:T(8,128)(2,1)S(1)} collective-permute-done((bf16[12,7168]{1,0:T(8,128)(2,1)S(1)}, bf16[12,7168]{1,0:T(8,128)(2,1)S(1)}, u32[]{:S(2)}, u32[]{:S(2)}) %collective-permute-start.3) | collective-permute-done | bytes 172064
  315.9 0.0 collective-permute-done
  315.9 0.0 collective-permute-done.1
  315.9 0.7 copy-done.2
  316.6 0.7 copy-done.1
  317.3 0.0 collective-permute-done.2
  317.3 7.8 %concatenate = bf16[76,7168]{1,0:T(8,128)(2,1)S(1)} concatenate(bf16[12,7168]{1,0:T(8,128)(2,1)} %copy-done.2, bf16[16,7168]{1,0:T(8,128)(2,1)} %collective-permute-done.2, bf16[16,7168]{1,0:T(8,128)(2,1)} %copy-done.1, bf16[16,7168]{1,0:T(8,128)(2,1)S(1)} %collective-permute-done, bf16[16,7168]{1,0:T(8,128)(2,1)S(1)} %fusion), dimensions={0} | concatenate | bytes 2179072
  325.1 2.9 convolution_convert_fusion.1
  (6 shorter events, 0.0 us)
Async XLA Ops:
  6.5 1.5 copy-start
  6.5 82.2 %all-gather.9.cloned.1.call-start = ((), (), s32[]{:S(2)}) async-start(), calls=%async_computation.2 | async-start | bytes 3899392 | tf_op jit(solution)/shard_map/all_gather | solution.py:19
  9.1 141.6 %all-gather.5.cloned.1.call-start = ((), (), s32[]{:S(2)}) async-start(), calls=%async_computation | async-start | bytes 3784704 | tf_op jit(solution)/shard_map/all_gather | solution.py:20
  9.9 202.1 %all-gather.7.cloned.1.call-start = ((), (), s32[]{:S(2)}) async-start(), calls=%async_computation.1 | async-start | bytes 1892352 | tf_op jit(solution)/shard_map/all_gather | solution.py:21
  262.1 53.8 %collective-permute-start = (bf16[16,7168]{1,0:T(8,128)(2,1)S(1)}, bf16[16,7168]{1,0:T(8,128)(2,1)S(1)}, u32[]{:S(2)}, u32[]{:S(2)}) collective-permute-start(bf16[16,7168]{1,0:T(8,128)(2,1)S(1)} %fusion), channel_id=1, source_target_pairs={{0,1},{1,2},{2,3},{3,4},{4,5},{5,6},{6,7},{7,8},{8,9},{9,10},{10,1... | collective-permute-start | bytes 688136
  267.6 48.4 %collective-permute-start.1 = (bf16[16,7168]{1,0:T(8,128)(2,1)S(1)}, bf16[16,7168]{1,0:T(8,128)(2,1)S(1)}, u32[]{:S(2)}, u32[]{:S(2)}) collective-permute-start(bf16[16,7168]{1,0:T(8,128)(2,1)S(1)} %fusion), channel_id=1, source_target_pairs={{0,2},{1,3},{2,4},{3,5},{4,6},{5,7},{6,8},{7,9},{8,10},{9,11},{10,... | collective-permute-start | bytes 688136
  270.0 47.4 %collective-permute-start.2 = (bf16[16,7168]{1,0:T(8,128)(2,1)S(1)}, bf16[16,7168]{1,0:T(8,128)(2,1)}, u32[]{:S(2)}, u32[]{:S(2)}) collective-permute-start(bf16[16,7168]{1,0:T(8,128)(2,1)S(1)} %fusion), channel_id=1, source_target_pairs={{0,3},{1,4},{2,5},{3,6},{4,7},{5,8},{6,9},{7,10},{8,11},{9,12},{10... | collective-permute-start | bytes 688136
  276.7 39.2 %collective-permute-start.3 = (bf16[12,7168]{1,0:T(8,128)(2,1)S(1)}, bf16[12,7168]{1,0:T(8,128)(2,1)S(1)}, u32[]{:S(2)}, u32[]{:S(2)}) collective-permute-start(bf16[12,7168]{1,0:T(8,128)(2,1)S(1)} %slice.10), channel_id=1, source_target_pairs={{0,4},{1,5},{2,6},{3,7},{4,8},{5,9},{6,10},{7,11},{8,12},{9,13},{1... | collective-permute-start | bytes 516104
  315.9 0.7 copy-start.2
  316.6 0.7 copy-start.1
Sparse Core Ops, SparseCore 0:
  9.4 79.3 all-gather.8
  92.0 58.7 all-gather.4
  153.9 58.0 all-gather.6
